TPU v7x, 768 devices: a whole 4x8x12 slice. The times are simulated.
768 devices in a mesh: dp: 48 (over z, y_hi), row: 4 (over x), col: 4 (over y_lo, core).
Axes of the slice: x: 4, y: 8 (y_hi: 4, y_lo: 2; y = y_hi * 2 + y_lo), z: 12, core: 2. Of those that a mesh axis runs over, the one named last changes fastest.
Arguments:
- inputs: float32 [12288, 6144], P('dp', 'row'), may hold values from -6 to 6
- out_grad: float32 [12288, 2048], P('dp', 'col'), may hold values from -6 to 6
- weight: float32 [6144, 2048], P(('row', 'dp'), 'col'), may hold values from -0.078125 to 0.078125
- moment_mean: float32 [6144, 2048], P(('row', 'dp'), 'col'), may hold values from -6 to 6
- moment_square: float32 [6144, 2048], P(('row', 'dp'), 'col'), may hold values from 0.5 to 2
Outputs:
- outputs: float32 [12288, 2048], P(('dp', 'row'), 'col')
- in_grad: float32 [12288, 6144], P(('dp', 'col'), 'row')
- new_weight: float32 [6144, 2048], P(('row', 'dp'), 'col')
- new_mean: float32 [6144, 2048], P(('row', 'dp'), 'col')
- new_square: float32 [6144, 2048], P(('row', 'dp'), 'col')
All inputs are finite; a program needn't handle non-finite values.
Results may differ from a plain program's by a relative error of at most 0.00007.
Values sent between devices are 32-bit elements; how exact they have to be, the bound alone decides.
A program may use at most 32 MiB of HBM per device.

v0:
```python
import math

import jax
import jax.numpy as jnp
from jax import lax
from jax.sharding import Mesh
from jax.sharding import PartitionSpec as P

STEP = 10
DP = ("dp_0", "dp_1")
ROW_DP = ("row", "dp_0", "dp_1")
DP_ROW = ("dp_0", "dp_1", "row")
DP_COL = ("dp_0", "dp_1", "col")


def cut_along(array, dim, count):
    dims = array.shape
    tiles = array.reshape(*dims[:dim], count, dims[dim] // count, *dims[dim + 1 :])
    return jnp.moveaxis(tiles, dim, 0)


def summed_on_arrival(array, axis, dim):
    count = lax.axis_size(axis)
    tiles = lax.all_to_all(cut_along(array, dim, count), axis, 0, 0, tiled=True)
    return jnp.sum(tiles, axis=0)


def sum_by_axis(subtotal, axes):
    for axis in axes:
        subtotal = lax.psum_scatter(subtotal, axis, scatter_dimension=0, tiled=True)
    return subtotal


def adamw_update(weight, moment_mean, moment_square, gradient):
    new_mean = 0.9 * moment_mean + 0.1 * gradient
    new_square = 0.95 * moment_square + 0.05 * gradient * gradient
    mean_hat = new_mean / (1.0 - 0.9**STEP)
    square_hat = new_square / (1.0 - 0.95**STEP)
    new_weight = weight - 0.02 * (mean_hat / (jnp.sqrt(square_hat) + 1e-08) + 0.1 * weight)
    return (new_weight, new_mean, new_square)


def per_device(inputs, out_grad, weight, moment_mean, moment_square):
    highest = lax.Precision.HIGHEST
    weight_tile = lax.all_gather(weight, DP, axis=0, tiled=True)
    partial_out = jnp.dot(
        inputs, weight_tile, precision=highest, preferred_element_type=jnp.float32
    )
    partial_in = lax.dot_general(
        out_grad,
        weight_tile,
        (((1,), (1,)), ((), ())),
        precision=highest,
        preferred_element_type=jnp.float32,
    )
    outputs = summed_on_arrival(partial_out, "row", 0)
    in_grad = lax.psum_scatter(partial_in, "col", scatter_dimension=0, tiled=True)
    token_count = inputs.shape[0] * lax.axis_size(DP)
    factor = 1.0 / math.sqrt(token_count)
    product = lax.dot_general(
        inputs,
        out_grad,
        (((0,), (0,)), ((), ())),
        precision=highest,
        preferred_element_type=jnp.float32,
    )
    gradient = sum_by_axis(product, DP) * factor
    new_weight, new_mean, new_square = adamw_update(weight, moment_mean, moment_square, gradient)
    return (outputs, in_grad, new_weight, new_mean, new_square)


def solution(mesh):
    split = Mesh(
        mesh.devices.reshape(12, 4, mesh.shape["row"], mesh.shape["col"]),
        ("dp_0", "dp_1", "row", "col"),
    )
    placed = (P(DP, "row"), P(DP, "col"), P(ROW_DP, "col"), P(ROW_DP, "col"), P(ROW_DP, "col"))
    return jax.shard_map(
        per_device,
        mesh=split,
        in_specs=placed,
        out_specs=(
            P(DP_ROW, "col"),
            P(DP_COL, "row"),
            P(ROW_DP, "col"),
            P(ROW_DP, "col"),
            P(ROW_DP, "col"),
        ),
        check_vma=False,
    )
```

profile of v0, /device:TPU:6, one launch (start us, length us, event | category | flops | bytes accessed | tf_op | source)
XLA Modules:
  0.0 197.7 jit_solution(14474579036086898270)
XLA Ops:
  8.0 0.0 copy-start
  8.0 0.0 copy-start.1
  8.0 0.0 reduce-scatter.6.cloned.1.call-start
  8.1 1.3 copy-done
  9.4 5.4 %fusion.2 = f32[1536,512]{1,0:T(8,128)} fusion(f32[256,1536]{1,0:T(8,128)S(1)} %copy-done, f32[256,512]{1,0:T(8,128)} %param.6), kind=kOutput, calls=%fused_computation.5 | convolution fusion | flops 2415919104 | bytes 5242880 | tf_op jit(solution)/shard_map/dot_general | solution.py:60
  14.8 0.0 reduce-scatter.6.cloned.1.call-update
  14.8 0.0 all-gather.2.cloned.1.call-start
  14.9 0.5 all-gather.2.cloned.1.call-update
  15.4 0.0 reduce-scatter.8.cloned.1.call-start
  15.4 72.4 %reduce-scatter.6.cloned.1.call-done = f32[128,512]{1,0:T(8,128)} async-done(((f32[1536,512]{1,0:T(8,128)}), f32[128,512]{1,0:T(8,128)}) %reduce-scatter.6.cloned.1.call-update) | async-done | bytes 262160 | tf_op jit(solution)/shard_map/reduce_scatter | solution.py:30
  87.8 0.0 reduce-scatter.8.cloned.1.call-update
  87.8 0.0 reduce-scatter.4.cloned.1.call-start
  87.9 66.9 %all-gather.2.cloned.1.call-done = f32[1536,512]{1,0:T(8,128)} async-done(((f32[32,512]{1,0:T(8,128)}), f32[1536,512]{1,0:T(8,128)}) %all-gather.2.cloned.1.call-update) | async-done | bytes 3145744 | tf_op jit(solution)/shard_map/all_gather | solution.py:45
  154.8 0.0 copy-done.1
  154.8 5.8 %fusion.1 = f32[256,1536]{1,0:T(8,128)} fusion(f32[256,512]{1,0:T(8,128)S(1)} %copy-done.1, f32[1536,512]{1,0:T(8,128)} %all-gather.2.cloned.1.call-done), kind=kOutput, calls=%fused_computation.4 | convolution fusion | flops 2415919104 | bytes 5242880 | tf_op jit(solution)/shard_map/dot_general | solution.py:49
  160.6 0.0 reduce-scatter.4.cloned.1.call-update
  160.7 0.0 copy-start.2
  160.7 0.0 copy-start.3
  160.7 0.0 copy-start.4
  160.7 4.7 %fusion = f32[256,512]{1,0:T(8,128)S(1)} fusion(f32[256,1536]{1,0:T(8,128)S(1)} %copy-done, f32[1536,512]{1,0:T(8,128)} %all-gather.2.cloned.1.call-done), kind=kOutput, calls=%fused_computation.3 | convolution fusion | flops 2415919104 | bytes 5242880 | tf_op jit(solution)/shard_map/dot_general | solution.py:46
  165.4 10.5 %all_to_all.5 = f32[4,64,512]{2,1,0:T(8,128)S(1)} all-to-all(f32[4,64,512]{2,1,0:T(8,128)S(1)} %bitcast.7), channel_id=1, replica_groups=mesh['dp_0'=12,'dp_1'=4,'row'=4,'col'=4] {'row'}, dimensions={0} | all-to-all | bytes 1048576 | tf_op jit(solution)/shard_map/all_to_all | solution.py:24
  176.0 0.7 reduce_sum.9
  176.7 0.0 reduce-scatter.8.cloned.1.call-done
  176.7 0.0 copy-done.2
  176.7 0.0 copy-done.3
  176.7 0.0 copy-done.4
  176.7 1.5 multiply_subtract_fusion
  178.2 12.4 %reduce-scatter.4.cloned.1.call-done = f32[64,1536]{1,0:T(8,128)} async-done(((f32[256,1536]{1,0:T(8,128)}), f32[64,1536]{1,0:T(8,128)}) %reduce-scatter.4.cloned.1.call-update) | async-done | bytes 393232 | tf_op jit(solution)/shard_map/reduce_scatter | solution.py:57
Async XLA Ops:
  8.0 1.4 copy-start
  8.0 146.8 %copy-start.1 = (f32[256,512]{1,0:T(8,128)S(1)}, f32[256,512]{1,0:T(8,128)}, u32[]{:S(2)}) copy-start(f32[256,512]{1,0:T(8,128)} %param.6) | copy-start | bytes 1572868
  8.0 79.8 %reduce-scatter.6.cloned.1.call-start = ((), (), s32[]{:S(2)}) async-start(), calls=%async_computation.6 | async-start | bytes 3407872 | tf_op jit(solution)/shard_map/reduce_scatter | solution.py:30
  14.8 140.0 %all-gather.2.cloned.1.call-start = ((), (), s32[]{:S(2)}) async-start(), calls=%async_computation.4 | async-start | bytes 3211264 | tf_op jit(solution)/shard_map/all_gather | solution.py:45
  15.4 161.3 %reduce-scatter.8.cloned.1.call-start = ((), (), s32[]{:S(2)}) async-start(), calls=%async_computation.7 | async-start | bytes 327680 | tf_op jit(solution)/shard_map/reduce_scatter | solution.py:30
  87.8 102.8 %reduce-scatter.4.cloned.1.call-start = ((), (), s32[]{:S(2)}) async-start(), calls=%async_computation.5 | async-start | bytes 1966080 | tf_op jit(solution)/shard_map/reduce_scatter | solution.py:57
  160.7 16.0 %copy-start.2 = (f32[32,512]{1,0:T(8,128)S(1)}, f32[32,512]{1,0:T(8,128)}, u32[]{:S(2)}) copy-start(f32[32,512]{1,0:T(8,128)} %param.7) | copy-start | bytes 196612
  160.7 16.0 %copy-start.3 = (f32[32,512]{1,0:T(8,128)S(1)}, f32[32,512]{1,0:T(8,128)}, u32[]{:S(2)}) copy-start(f32[32,512]{1,0:T(8,128)} %param.8) | copy-start | bytes 196612
  160.7 16.0 %copy-start.4 = (f32[32,512]{1,0:T(8,128)S(1)}, f32[32,512]{1,0:T(8,128)}, u32[]{:S(2)}) copy-start(f32[32,512]{1,0:T(8,128)} %param.9) | copy-start | bytes 196612
Sparse Core Ops, SparseCore 0:
  14.9 72.8 reduce-scatter.5
  90.9 43.8 reduce-scatter.7
  160.8 29.7 reduce-scatter.3
Sparse Core Ops, SparseCore 1:
  18.9 135.9 all-gather.1
where the time goes:
time: 199 us; the launch traced here: 198 us
  waiting for transfers between devices  152 us (76%)
  matrix products  15.9 us (8%)
  between operations  15.2 us (8%)
  blocking collectives  10.5 us (5%)
  other arithmetic  2.23 us (1%)
    reduce_scatter x2, waiting for transfers between devices, sum_by_axis(): subtotal = lax.psum_scatter(subtotal, axis, scatter_dimension=0, tiled=True)  72.4 us
    all_gather x1, waiting for transfers between devices, per_device(): weight_tile = lax.all_gather(weight, DP, axis=0, tiled=True)  66.9 us
    reduce_scatter x1, waiting for transfers between devices, per_device(): lax.psum_scatter(partial_in, 'col', scatter_dimension=0, tiled=True)  12.4 us
    all_to_all x1, blocking collectives, summed_on_arrival(): tiles = lax.all_to_all(cut_along(array, dim, count), axis, 0, 0, tiled=True)  10.5 us
    dot_general x1, matrix products, per_device(): lax.dot_general(out_grad, weight_tile, (((1,), (1,)), ((), ())), precisio...  5.83 us
    dot_general x1, matrix products, per_device(): lax.dot_general(inputs, out_grad, (((0,), (0,)), ((), ())), precision=hig...  5.38 us
    dot_general x1, matrix products, per_device(): jnp.dot(inputs, weight_tile, precision=highest, preferred_element_type=jn...  4.74 us
  transfers between devices with their start and end apart: 4, of which 3 were waited for; matrix products, arithmetic and copies ran while one was open for 6% of the time, Pallas kernels for 0%

commit v1 on v0

v1 whole, which is shorter than its diff:
```python
import math

import jax
import jax.numpy as jnp
from jax import lax
from jax.experimental import pallas as pl
from jax.experimental.pallas import tpu as pltpu
from jax.sharding import Mesh
from jax.sharding import PartitionSpec as P

STEP = 10
NZ, NH, NX = 12, 4, 4
HALF = NZ // 2
ORDER = (0, 1, 3, 2)
LAST = ((0, 1), (3, 2))
MESH = pl.DeviceIdType.MESH
ROWS = 32
SLAB = NH * ROWS
F32 = jnp.float32
BF16 = jnp.bfloat16


def halves(value):
    high = value.astype(BF16)
    low = (value - high.astype(F32)).astype(BF16)
    return high, low


def dot3(a, b, dims):
    (ah, al), (bh, bl) = a, b

    def one(p, q):
        return lax.dot_general(p, q, (dims, ((), ())), preferred_element_type=F32)

    return one(ah, bh) + (one(ah, bl) + one(al, bh))


def kernel(
    in_ref, og_ref, w_ref, mm_ref, ms_ref,
    out_ref, ig_ref, nw_ref, nm_ref, ns_ref,
    wt, rs, first, prod, total, hland, pout, xland, pin, cland, yland,
    in_hi, in_lo, og_hi, og_lo,
    h_s, h_r, ag_s, ag_r, rs_s, rs_r, c_s, c_r, y_s, y_r, x_s, x_r, g_s, g_r,
):
    z, h, x = lax.axis_index("z"), lax.axis_index("h"), lax.axis_index("x")
    l, c = lax.axis_index("l"), lax.axis_index("c")

    def around(at, by, n):
        return lax.rem(at + by + n, n)

    def to(axis, at, by, n):
        return {axis: around(at, by, n)}

    def copy(src, dst, s, r, dev):
        return pltpu.make_async_remote_copy(
            src_ref=src, dst_ref=dst, send_sem=s, recv_sem=r, device_id=dev, device_id_type=MESH
        )

    partners = [to("z", z, 1, NZ), to("z", z, -1, NZ), {"c": 1 - c}, {"l": 1 - l}]
    partners += [to("h", h, j, NH) for j in (1, 2, 3)] + [to("x", x, j, NX) for j in (1, 2, 3)]
    barrier = pltpu.get_barrier_semaphore()
    for dev in partners:
        pl.semaphore_signal(barrier, inc=1, device_id=dev, device_id_type=MESH)
    pl.semaphore_wait(barrier, len(partners))

    def rows_of(zz, hh):
        return pl.ds(pl.multiple_of((zz * NH + hh) * ROWS, ROWS), ROWS)

    def slab_at(zz):
        return pl.ds(pl.multiple_of(zz * SLAB, SLAB), SLAB)

    def sign(d):
        return 1 - 2 * d

    def h_copy(j):
        return copy(w_ref, wt.at[rows_of(z, h)], h_s.at[j - 1], h_r.at[j - 1], to("h", h, j, NH))

    def ag_copy(d, i, k, src=None):
        zz = around(z, -sign(d) * i, NZ)
        here = wt.at[rows_of(zz, around(h, -k, NH))]
        return copy(here if src is None else src, here, ag_s.at[d, i, k], ag_r.at[d, i, k], to("z", z, sign(d), NZ))

    for d in (0, 1):
        ag_copy(d, 0, 0, w_ref).start()
    for j in (1, 3, 2):
        h_copy(j).start()
    wt[rows_of(z, h), :] = w_ref[...]

    og_hi[...], og_lo[...] = halves(og_ref[...])
    in_hi[...], in_lo[...] = halves(in_ref[...])
    og = lambda: (og_hi[...], og_lo[...])

    def product(zz):
        a = (in_hi[:, slab_at(zz)], in_lo[:, slab_at(zz)])
        return dot3(a, og(), ((0,), (0,)))

    def rs_copy(d, i, half, src):
        rows = pl.ds(half * 64, 64)
        return copy(src.at[rows], rs.at[d, i, rows], rs_s.at[d, i, half], rs_r.at[d, i, half], to("z", z, sign(d), NZ))

    first[...] = product(around(z, HALF, NZ))
    rs_copy(0, 0, 0, first).start()
    rs_copy(1, 0, 1, first).start()

    for k in (1, 3, 2):
        h_copy(k).wait_recv()
        for d in (0, 1):
            ag_copy(d, 0, k).start()

    def c_copy(zz):
        return copy(pin.at[zz, :, 1 - c], cland.at[zz], c_s.at[zz], c_r.at[zz], {"c": 1 - c})

    def y_copy(zz):
        return copy(pin.at[zz, 1 - l, c], yland.at[zz], y_s.at[zz], y_r.at[zz], {"l": 1 - l})

    def slab(zz, start):
        w = halves(wt[slab_at(zz), :])
        part = dot3(og(), w, ((1,), (1,)))
        pin[zz] = part.reshape(2, 2, 64, 128)
        c_copy(zz).start()
        out = dot3((in_hi[:, slab_at(zz)], in_lo[:, slab_at(zz)]), w, ((1,), (0,)))
        pout[...] = out if start else pout[...] + out

    def second(zz):
        c_copy(zz).wait_recv()
        c_copy(zz).wait_send()
        pin[zz, 1 - l, c] = pin[zz, 1 - l, c] + cland[zz, 1 - l]
        y_copy(zz).start()

    for d in (0, 1):
        prod[d] = product(around(z, sign(d) * (HALF - 1), NZ))
    slab(z, True)

    def tick(i, carry):
        for k in ORDER:
            for d in (0, 1):
                ag_copy(d, i - 1, k).wait_recv()
                if k in LAST[d]:
                    ag_copy(d, i, k).start()
                else:

                    @pl.when(i < HALF - 1)
                    def _():
                        ag_copy(d, i, k).start()

        for half in (0, 1):
            for d in (0, 1):
                rows = pl.ds(half * 64, 64)

                def add():
                    rs_copy(d, i - 1, half, first).wait_recv()
                    rs[d, i - 1, rows, :] = rs[d, i - 1, rows, :] + prod[d, rows, :]

                if half == d:
                    add()
                else:
                    pl.when(i > 1)(add)

                    @pl.when(i == 1)
                    def _():
                        rs[d, i - 1, rows, :] = prod[d, rows, :]

                rs_copy(d, i, half, rs.at[d, i - 1]).start()

        def each(d, carry):
            @pl.when(jnp.logical_or(i > 1, d == 0))
            def _():
                second(around(z, sign(d) * (1 - i), NZ))

            slab(around(z, -sign(d) * i, NZ), False)
            prod[d] = product(around(z, sign(d) * (HALF - 1 - i), NZ))
            return carry

        return lax.fori_loop(0, 2, each, carry)

    lax.fori_loop(1, HALF, tick, 0)

    far = around(z, HALF, NZ)
    for d in (0, 1):
        for k in LAST[d]:
            ag_copy(d, HALF - 1, k).wait_recv()
    slab(far, False)

    def x_copy(j):
        at = pl.ds(pl.multiple_of(around(x, j, NX) * 64, 64), 64)
        return copy(pout.at[at], xland.at[j - 1], x_s.at[j - 1], x_r.at[j - 1], to("x", x, j, NX))

    for j in (2, 1, 3):
        x_copy(j).start()

    for half in (0, 1):
        rows = pl.ds(half * 64, 64)
        for d in (0, 1):
            rs_copy(d, HALF - 1, half, first).wait_recv()
        total[rows, :] = prod[0, rows, :] + rs[0, HALF - 1, rows, :] + rs[1, HALF - 1, rows, :]

    def g_copy(j):
        at = pl.ds(pl.multiple_of(around(h, j, NH) * ROWS, ROWS), ROWS)
        return copy(total.at[at], hland.at[j - 1], g_s.at[j - 1], g_r.at[j - 1], to("h", h, j, NH))

    for j in (2, 1, 3):
        g_copy(j).start()

    second(around(z, 1 - HALF, NZ))
    second(around(z, HALF - 1, NZ))
    second(far)

    def finish(zz, carry):
        y_copy(zz).wait()
        at = pl.ds(pl.multiple_of(zz * 128, 128), 128)
        ig_ref[:, at] = pin[zz, l, c] + cland[zz, l] + yland[zz]
        return carry

    lax.fori_loop(0, NZ, finish, 0)

    for j in (1, 2, 3):
        x_copy(j).wait()
    out_ref[...] = (
        pout[pl.ds(pl.multiple_of(x * 64, 64), 64), :] + xland[0] + (xland[1] + xland[2])
    )

    for j in (1, 2, 3):
        g_copy(j).wait()
    summed = total[pl.ds(pl.multiple_of(h * ROWS, ROWS), ROWS), :] + hland[0] + (hland[1] + hland[2])
    gradient = summed * (1.0 / math.sqrt(NZ * NH * 256))
    new_mean = 0.9 * mm_ref[...] + 0.1 * gradient
    new_square = 0.95 * ms_ref[...] + 0.05 * gradient * gradient
    mean_hat = new_mean / (1.0 - 0.9**STEP)
    square_hat = new_square / (1.0 - 0.95**STEP)
    weight = w_ref[...]
    nw_ref[...] = weight - 0.02 * (mean_hat / (jnp.sqrt(square_hat) + 1e-08) + 0.1 * weight)
    nm_ref[...] = new_mean
    ns_ref[...] = new_square

    for j in (1, 2, 3):
        h_copy(j).wait_send()

    def drain(i, carry):
        for d in (0, 1):
            for k in ORDER:
                if k in LAST[d]:
                    ag_copy(d, i, k).wait_send()
                else:

                    @pl.when(i < HALF - 1)
                    def _():
                        ag_copy(d, i, k).wait_send()

            for half in (0, 1):

                def done():
                    rs_copy(d, i, half, first).wait_send()

                if half == d:
                    done()
                else:
                    pl.when(i > 0)(done)
        return carry

    lax.fori_loop(0, HALF, drain, 0)


def per_device(inputs, out_grad, weight, moment_mean, moment_square):
    dma = pltpu.SemaphoreType.DMA
    shape = jax.ShapeDtypeStruct
    vmem = pl.BlockSpec(memory_space=pltpu.VMEM)
    small = shape((ROWS, 512), F32)
    return pl.pallas_call(
        kernel,
        out_shape=(shape((64, 512), F32), shape((64, 1536), F32), small, small, small),
        in_specs=[vmem] * 5,
        out_specs=[vmem] * 5,
        scratch_shapes=[
            pltpu.VMEM((1536, 512), F32),
            pltpu.VMEM((2, HALF, SLAB, 512), F32),
            pltpu.VMEM((SLAB, 512), F32),
            pltpu.VMEM((2, SLAB, 512), F32),
            pltpu.VMEM((SLAB, 512), F32),
            pltpu.VMEM((3, ROWS, 512), F32),
            pltpu.VMEM((256, 512), F32),
            pltpu.VMEM((3, 64, 512), F32),
            pltpu.VMEM((NZ, 2, 2, 64, 128), F32),
            pltpu.VMEM((NZ, 2, 64, 128), F32),
            pltpu.VMEM((NZ, 64, 128), F32),
            pltpu.VMEM((256, 1536), BF16),
            pltpu.VMEM((256, 1536), BF16),
            pltpu.VMEM((256, 512), BF16),
            pltpu.VMEM((256, 512), BF16),
            dma((3,)), dma((3,)),
            dma((2, HALF, 4)), dma((2, HALF, 4)),
            dma((2, HALF, 2)), dma((2, HALF, 2)),
            dma((NZ,)), dma((NZ,)),
            dma((NZ,)), dma((NZ,)),
            dma((3,)), dma((3,)),
            dma((3,)), dma((3,)),
        ],
        compiler_params=pltpu.CompilerParams(
            collective_id=0, has_side_effects=True, vmem_limit_bytes=48 << 20
        ),
        name="step",
    )(inputs, out_grad, weight, moment_mean, moment_square)


def solution(mesh):
    split = Mesh(mesh.devices.reshape(NZ, NH, NX, 2, 2), ("z", "h", "x", "l", "c"))
    tile = P(("x", "z", "h"), ("l", "c"))
    return jax.shard_map(
        per_device,
        mesh=split,
        in_specs=(P(("z", "h"), "x"), P(("z", "h"), ("l", "c")), tile, tile, tile),
        out_specs=(P(("z", "h", "x"), ("l", "c")), P(("z", "h", "l", "c"), "x"), tile, tile, tile),
        check_vma=False,
    )
```

time: 199 us -> 103 us (0.52)
  waiting for transfers between devices: 152 us -> 0 us
  Pallas kernels: 0 us -> 91.7 us
  matrix products: 15.9 us -> 0 us
  between operations: 15.2 us -> 0.66 us
  blocking collectives: 10.5 us -> 0 us
  local copies, waits for them, and re-layouts: 1.37 us -> 8.25 us
  other arithmetic: 2.23 us -> 0 us
    pallas_call x0 -> x1, Pallas kernels: none -> 91.7 us  [per_device(): pl.pallas_call(kernel, out_shape=(shape((64, 512), F32), shape((64, 1536)...]
    reduce_scatter x3 -> x0, waiting for transfers between devices: 84.7 us -> none  [the longest x2 72.4 us: sum_by_axis(): subtotal = lax.psum_scatter(subtotal, axis, scatter_dimension=0, tiled=True)]
    all_gather x1 -> x0, waiting for transfers between devices: 66.9 us -> none  [per_device(): weight_tile = lax.all_gather(weight, DP, axis=0, tiled=True)]
    dot_general x3 -> x0, matrix products: 15.9 us -> none  [the longest x1 5.83 us: per_device(): lax.dot_general(out_grad, weight_tile, (((1,), (1,)), ((), ())), precisio...]
    all_to_all x1 -> x0, blocking collectives: 10.5 us -> none  [summed_on_arrival(): tiles = lax.all_to_all(cut_along(array, dim, count), axis, 0, 0, tiled=True)]
    unnamed x10 -> x15, local copies, waits for them, and re-layouts: 1.37 us -> 8.25 us
  transfers between devices with their start and end apart: 4 -> 0, of which waited for: 3 -> 0; matrix products, arithmetic and copies ran while one was open for 6% -> 0% of each run, Pallas kernels for 0% -> 0%
where the time goes in v1:
time: 103 us; the launch traced here: 101 us
  Pallas kernels  91.7 us (89%)
  local copies, waits for them, and re-layouts  8.25 us (8%)
    pallas_call x1, Pallas kernels, per_device(): pl.pallas_call(kernel, out_shape=(shape((64, 512), F32), shape((64, 1536)...  91.7 us
    unnamed x15, local copies, waits for them, and re-layouts  8.25 us

profile of v1, /device:TPU:6, one launch (start us, length us, event | category | flops | bytes accessed | tf_op | source)
XLA Modules:
  0.0 100.6 jit_solution(5037140548315475363)
XLA Ops:
  0.6 0.0 copy-start
  0.6 1.4 %copy-done = f32[256,1536]{1,0:T(8,128)S(1)} copy-done((f32[256,1536]{1,0:T(8,128)S(1)}, f32[256,1536]{1,0:T(8,128)}, u32[]{:S(2)}) %copy-start) | copy-done | bytes 1572888
  2.0 0.0 copy-start.1
  2.0 1.0 %copy-done.1 = f32[256,512]{1,0:T(8,128)S(1)} copy-done((f32[256,512]{1,0:T(8,128)S(1)}, f32[256,512]{1,0:T(8,128)}, u32[]{:S(2)}) %copy-start.1) | copy-done | bytes 524312
  3.1 0.0 copy-start.2
  3.1 0.8 copy-done.2
  3.9 0.0 copy-start.3
  3.9 0.8 copy-done.3
  4.8 0.0 copy-start.4
  4.8 0.8 copy-done.4
  5.6 91.7 %step.1 = (f32[64,512]{1,0:T(8,128)S(1)}, f32[64,1536]{1,0:T(8,128)S(1)}, f32[32,512]{1,0:T(8,128)S(1)}, f32[32,512]{1,0:T(8,128)S(1)}, f32[32,512]{1,0:T(8,128)S(1)}) custom-call(f32[256,1536]{1,0:T(8,128)S(1)} %copy-done, f32[256,512]{1,0:T(8,128)S(1)} %copy-done.1, f32[32,512]{1,0:T(8,128)S(1)} %copy-done.2, f32[32,512]{1,0:T(8,128)S(1)} %copy-done.3, ...), custom_call_target="tpu_custom_call" | custom-call | tf_op jit(solution)/shard_map/step/pallas_call | solution.py:268
  97.3 0.7 copy.15
  98.0 0.7 copy.16
  98.7 0.6 copy.17
  99.4 0.6 copy.18
  100.0 0.6 copy.19
Async XLA Ops:
  0.6 1.4 %copy-start = (f32[256,1536]{1,0:T(8,128)S(1)}, f32[256,1536]{1,0:T(8,128)}, u32[]{:S(2)}) copy-start(f32[256,1536]{1,0:T(8,128)} %in_ref.1) | copy-start | bytes 4718596
  2.0 1.0 %copy-start.1 = (f32[256,512]{1,0:T(8,128)S(1)}, f32[256,512]{1,0:T(8,128)}, u32[]{:S(2)}) copy-start(f32[256,512]{1,0:T(8,128)} %og_ref.1) | copy-start | bytes 1572868
  3.1 0.8 copy-start.2
  3.9 0.8 copy-start.3
  4.8 0.8 copy-start.4

commit v2 on v0

v2 whole, which is shorter than its diff:
```python
import math

import jax
import jax.numpy as jnp
from jax import lax
from jax.experimental import pallas as pl
from jax.experimental.pallas import tpu as pltpu
from jax.sharding import Mesh
from jax.sharding import PartitionSpec as P

STEP = 10
NZ, NH, NX = 12, 4, 4
HALF = NZ // 2
ORDER = (0, 1, 3, 2)
LAST = ((0, 1), (3, 2))
MESH = pl.DeviceIdType.MESH
ROWS = 32
SLAB = NH * ROWS
COLS = 512
CA = 384
CB = COLS - CA
COPIES = 160
F32 = jnp.float32
BF16 = jnp.bfloat16


def halves(value):
    high = value.astype(BF16)
    low = (value - high.astype(F32)).astype(BF16)
    return high, low


def dot3(a, b, dims):
    (ah, al), (bh, bl) = a, b

    def one(p, q):
        return lax.dot_general(p, q, (dims, ((), ())), preferred_element_type=F32)

    return one(ah, bh) + (one(ah, bl) + one(al, bh))


def sign(d):
    return 1 - 2 * d


def place(d, i):
    return 1 + 4 * ((i - 1) // 2) + 2 * d + (i - 1) % 2


def kernel(
    in_hbm, og_hbm, w_hbm, mm_hbm, ms_hbm,
    out_hbm, ig_hbm, nw_hbm, nm_hbm, ns_hbm,
    out_ref, ig_ref, nw_ref, nm_ref, ns_ref,
    w0, wa, wb, pa, pb, rs, far_l, near_l, q, zb, total, tg, ga, pout, tx, xl, pin, cland, yland,
    in_v, og_v, w_v, mm_v, ms_v, in_hi, in_lo, og_hi, og_lo,
    l_sem, o_sem, s_sem, r_sem, c_s, c_r, y_s, y_r,
):
    z, h, x = lax.axis_index("z"), lax.axis_index("h"), lax.axis_index("x")
    l, c = lax.axis_index("l"), lax.axis_index("c")

    def around(at, by, n):
        return lax.rem(at + by + n, n)

    def zto(by):
        return {"z": around(z, by, NZ)}

    def hto(by):
        return {"h": around(h, by, NH)}

    def xto(by):
        return {"x": around(x, by, NX)}

    def remote(src, dst, s, r, dev):
        return pltpu.make_async_remote_copy(
            src_ref=src, dst_ref=dst, send_sem=s, recv_sem=r, device_id=dev, device_id_type=MESH
        )

    made = []

    def copy(src, dst, dev):
        made.append(remote(src, dst, s_sem.at[len(made)], r_sem.at[len(made)], dev))
        return made[-1]

    loads = [
        pltpu.make_async_copy(a, b, l_sem.at[n])
        for n, (a, b) in enumerate(
            ((w_hbm, w_v), (og_hbm, og_v), (in_hbm, in_v), (mm_hbm, mm_v), (ms_hbm, ms_v))
        )
    ]
    for load in loads:
        load.start()

    partners = [zto(1), zto(-1), {"c": 1 - c}, {"l": 1 - l}]
    partners += [hto(j) for j in (1, 2, 3)] + [xto(j) for j in (1, -1)]
    barrier = pltpu.get_barrier_semaphore()
    for dev in partners:
        pl.semaphore_signal(barrier, inc=1, device_id=dev, device_id_type=MESH)
    pl.semaphore_wait(barrier, len(partners))

    def zz_at(by):
        return around(z, by, NZ)

    def rows_of(hh):
        return pl.ds(pl.multiple_of(hh * ROWS, ROWS), ROWS)

    def lanes_of(zz):
        return pl.ds(pl.multiple_of(zz * SLAB, SLAB), SLAB)

    cols_a, cols_b = pl.ds(0, CA), pl.ds(CA, CB)

    own_h = {j: copy(w_hbm, w0.at[rows_of(h)], hto(j)) for j in (1, 3, 2)}
    ag = {}
    for i in range(HALF):
        for d in (0, 1):
            zz = zz_at(-sign(d) * i)
            for k in ORDER:
                if i < HALF - 1 or k in LAST[d]:
                    at = rows_of(around(h, -k, NH))
                    src = wa.at[zz, at]
                    if i == 0:
                        src = w_hbm.at[:, cols_a] if k == 0 else w0.at[at, cols_a]
                    ag[d, i, k] = copy(src, wa.at[zz, at], zto(sign(d)))

    bz = {}
    for i in range(HALF):
        for d in (0, 1):
            if i < HALF - 1 or d == 0:
                src = w_hbm.at[:, cols_b] if i == 0 else wb.at[h, place(d, i)]
                bz[d, i] = copy(src, wb.at[h, place(d, i + 1)], zto(sign(d)))
    bh, bf = {}, {}
    for b in range(3):
        n = 4 if b < 2 else 3
        for d in (0, 1):
            at = pl.ds(1 + 4 * b, n)
            bh[b, d] = copy(wb.at[h, at], wb.at[h, at], hto(sign(d)))
            at = pl.ds(1 + 4 * b + 2 * d, 2 if d == 0 else n - 2)
            back = around(h, -sign(d), NH)
            bf[b, d] = copy(wb.at[back, at], wb.at[back, at], hto(sign(d)))

    def bhop(i):
        for d in (0, 1):
            if (d, i - 1) in bz:
                bz[d, i - 1].wait_recv()
                if (d, i) in bz:
                    bz[d, i].start()

    rsa = {}
    for i in range(HALF):
        for d in (0, 1):
            for half in (0, 1):
                if i > 0 or half == d:
                    at = pl.ds(half * 64, 64)
                    src = pa.at[0, at] if i == 0 else rs.at[d, i - 1, at]
                    rsa[d, i, half] = copy(src, rs.at[d, i, at], zto(sign(d)))

    groups = (pl.ds(0, HALF), pl.ds(HALF, HALF))
    two = around(h, 2, NH)
    g_far = {d: copy(pb.at[two, groups[d]], far_l.at[d], hto(sign(d))) for d in (0, 1)}
    g_near = {}
    for d in (0, 1):
        to = around(h, sign(d), NH)
        for g in (0, 1):
            g_near[d, g] = copy(pb.at[to, groups[g]], near_l.at[d, groups[g]], hto(sign(d)))
    rz = {}
    for j in range(HALF):
        for d in (0, 1):
            if j >= d:
                src = q.at[0 if d == 0 else NZ - 1] if j == d else zb.at[d, j - 1]
                rz[d, j] = copy(src, zb.at[d, j], zto(sign(d)))

    def rhop(j):
        for d in (0, 1):
            if j < d:
                continue
            if j > d:
                rz[d, j - 1].wait_recv()
                zb[d, j - 1] = zb[d, j - 1] + q[j if d == 0 else NZ - j]
            rz[d, j].start()

    for d in (0, 1):
        ag[d, 0, 0].start()
        bz[d, 0].start()
    for j in (1, 3, 2):
        own_h[j].start()

    for load in loads[:3]:
        load.wait()
    w0[rows_of(h), :] = w_v[...]
    og_hi[...], og_lo[...] = halves(og_v[...])
    in_hi[...], in_lo[...] = halves(in_v[...])

    def og():
        return og_hi[...], og_lo[...]

    def product(s):
        at = lanes_of(zz_at(HALF - s))
        part = dot3((in_hi[:, at], in_lo[:, at]), og(), ((0,), (0,)))
        pa[s] = part[:, :CA]
        pb[:, s] = part[:, CA:].reshape(NH, ROWS, CB)

    def c_copy(zz):
        return remote(pin.at[zz, :, 1 - c], cland.at[zz], c_s.at[zz], c_r.at[zz], {"c": 1 - c})

    def y_copy(zz):
        return remote(pin.at[zz, 1 - l, c], yland.at[zz], y_s.at[zz], y_r.at[zz], {"l": 1 - l})

    def multiply(zz, tile, start):
        w = halves(tile)
        part = dot3(og(), w, ((1,), (1,)))
        pin[zz] = part.reshape(2, 2, 64, 128)
        c_copy(zz).start()
        at = lanes_of(zz)
        out = dot3((in_hi[:, at], in_lo[:, at]), w, ((1,), (0,)))
        pout[...] = out if start else pout[...] + out

    def slab(by, at):
        zz = zz_at(by)
        tile = jnp.concatenate([wa[zz], wb[:, at].reshape(SLAB, CB)], axis=1)
        multiply(zz, tile, False)

    def slabs(first, last):
        def each(n, carry):
            i, d = first + n // 2, n % 2
            slab((2 * d - 1) * i, 1 + 4 * ((i - 1) // 2) + 2 * d + (i - 1) % 2)
            return carry

        lax.fori_loop(0, 2 * (last - first + 1), each, 0)

    def second(zz):
        c_copy(zz).wait_recv()
        c_copy(zz).wait_send()
        pin[zz, 1 - l, c] = pin[zz, 1 - l, c] + cland[zz, 1 - l]
        y_copy(zz).start()

    def seconds(first, last):
        def each(n, carry):
            second(zz_at((2 * (n % 2) - 1) * (first + n // 2)))
            return carry

        lax.fori_loop(0, 2 * (last - first + 1), each, 0)

    def ag_step(i, k):
        for d in (0, 1):
            if (d, i - 1, k) in ag:
                ag[d, i - 1, k].wait_recv()
                if (d, i, k) in ag:
                    ag[d, i, k].start()

    def rs_step(i):
        for half in (0, 1):
            for d in (0, 1):
                at = pl.ds(half * 64, 64)
                mine = pa[i if d == 0 else NZ - i, at, :]
                if (d, i - 1, half) in rsa:
                    rsa[d, i - 1, half].wait_recv()
                    rs[d, i - 1, at, :] = rs[d, i - 1, at, :] + mine
                else:
                    rs[d, i - 1, at, :] = mine
                rsa[d, i, half].start()

    product(0)
    rsa[0, 0, 0].start()
    rsa[1, 0, 1].start()
    for n, k in enumerate((1, 3, 2)):
        own_h[k].wait_recv()
        for d in (0, 1):
            ag[d, 0, k].start()
        product(1 + n)
        product(NZ - 1 - n)
    bhop(1)
    ag_step(1, 0)
    ag_step(1, 1)
    product(4)
    product(8)
    ag_step(1, 3)
    ag_step(1, 2)
    rs_step(1)
    bhop(2)
    for d in (0, 1):
        bh[0, d].start()
    product(5)
    product(7)
    product(6)
    for d in (0, 1):
        g_far[d].start()
    for d in (0, 1):
        g_near[d, 1 - d].start()
    multiply(z, w0[...], True)

    for i in range(2, HALF):
        if i <= 3:
            bhop(2 * i - 1)
        if i <= 4:
            for d in (0, 1):
                bh[i - 2, d].wait_recv()
                bf[i - 2, d].start()
        if i == 3:
            for d in (0, 1):
                for g in (0, 1):
                    g_near[d, g].wait_recv()
            g_near[0, 0].wait_send()
            g_near[1, 1].wait_send()
            q[...] = pb[h] + near_l[0] + near_l[1]
        if i >= 3:
            rhop(2 * (i - 3))
        for k in ORDER:
            ag_step(i, k)
        rs_step(i)
        if i == 2:
            for d in (0, 1):
                g_far[d].wait_recv()
                to = around(h, sign(d), NH)
                pb[to, groups[d]] = pb[to, groups[d]] + far_l[d]
                g_near[d, d].start()
        if i <= 3:
            bhop(2 * i)
            for d in (0, 1):
                bh[i - 1, d].start()
        if i >= 3:
            rhop(2 * (i - 3) + 1)
            for d in (0, 1):
                bf[i - 3, d].wait_recv()
        if i == 3:
            second(z)
            slabs(1, 2)
        if i == 4:
            seconds(1, 2)
            slabs(3, 4)
        if i == 5:
            seconds(3, 4)
            slabs(5, 5)

    for k in ORDER:
        ag_step(HALF, k)
    slab(HALF, place(0, HALF))

    def block(by):
        return pl.ds(pl.multiple_of(around(x, by, NX) * 64, 64), 64)

    sides = (pl.ds(0, 256), pl.ds(256, 256))
    x_far = {d: copy(pout.at[block(2), sides[d]], tx.at[d], xto(sign(d))) for d in (0, 1)}
    x_near = {}
    for d in (0, 1):
        for g in (0, 1):
            x_near[d, g] = copy(
                pout.at[block(sign(d)), sides[g]], xl.at[d, :, sides[g]], xto(sign(d))
            )
    for d in (0, 1):
        x_far[d].start()
    for d in (0, 1):
        x_near[d, 1 - d].start()

    for half in (0, 1):
        at = pl.ds(half * 64, 64)
        for d in (0, 1):
            rsa[d, HALF - 1, half].wait_recv()
        total[at, :] = pa[HALF, at, :] + rs[0, HALF - 1, at, :] + rs[1, HALF - 1, at, :]

    def part_of(by, g):
        return pl.ds(pl.multiple_of(around(h, by, NH) * ROWS + g * 16, 16), 16)

    t_far = {d: copy(total.at[part_of(2, d)], tg.at[d], hto(sign(d))) for d in (0, 1)}
    t_near = {}
    for d in (0, 1):
        for g in (0, 1):
            t_near[d, g] = copy(
                total.at[part_of(sign(d), g)], ga.at[d, pl.ds(g * 16, 16)], hto(sign(d))
            )
    for d in (0, 1):
        t_far[d].start()
    for d in (0, 1):
        t_near[d, 1 - d].start()

    far = zz_at(HALF)
    seconds(5, 5)
    second(far)

    for d in (0, 1):
        x_far[d].wait_recv()
        pout[block(sign(d)), sides[d]] = pout[block(sign(d)), sides[d]] + tx[d]
        x_near[d, d].start()
    for d in (0, 1):
        t_far[d].wait_recv()
        total[part_of(sign(d), d), :] = total[part_of(sign(d), d), :] + tg[d]
        t_near[d, d].start()

    def finish(zz, carry):
        y_copy(zz).wait()
        at = lanes_of(zz)
        ig_ref[:, at] = pin[zz, l, c] + cland[zz, l] + yland[zz]
        return carry

    lax.fori_loop(0, NZ, finish, 0)
    stores = [
        pltpu.make_async_copy(a, b, o_sem.at[n])
        for n, (a, b) in enumerate(
            ((ig_ref, ig_hbm), (out_ref, out_hbm), (nw_ref, nw_hbm), (nm_ref, nm_hbm), (ns_ref, ns_hbm))
        )
    ]
    stores[0].start()
    for load in loads[3:]:
        load.wait()

    def adamw(cols, summed):
        gradient = summed * (1.0 / math.sqrt(NZ * NH * 256))
        new_mean = 0.9 * mm_v[:, cols] + 0.1 * gradient
        new_square = 0.95 * ms_v[:, cols] + 0.05 * gradient * gradient
        mean_hat = new_mean / (1.0 - 0.9**STEP)
        square_hat = new_square / (1.0 - 0.95**STEP)
        weight = w_v[:, cols]
        nw_ref[:, cols] = weight - 0.02 * (mean_hat / (jnp.sqrt(square_hat) + 1e-08) + 0.1 * weight)
        nm_ref[:, cols] = new_mean
        ns_ref[:, cols] = new_square

    for d in (0, 1):
        rz[d, HALF - 1].wait_recv()
    adamw(cols_b, q[HALF] + zb[0, HALF - 1] + zb[1, HALF - 1])

    for d in (0, 1):
        for g in (0, 1):
            x_near[d, g].wait_recv()
    out_ref[...] = pout[block(0), :] + xl[0] + xl[1]
    stores[1].start()

    for d in (0, 1):
        for g in (0, 1):
            t_near[d, g].wait_recv()
    adamw(cols_a, total[rows_of(h), :] + ga[0] + ga[1])
    for store in stores[2:]:
        store.start()

    for one in made:
        if one is not g_near[0, 0] and one is not g_near[1, 1]:
            one.wait_send()
    for store in stores:
        store.wait()


def write(*refs):
    srcs, dsts, held, l_sem, o_sem = refs[:5], refs[5:10], refs[10:15], refs[15], refs[16]
    loads = [pltpu.make_async_copy(a, b, l_sem.at[n]) for n, (a, b) in enumerate(zip(srcs, held))]
    stores = [pltpu.make_async_copy(a, b, o_sem.at[n]) for n, (a, b) in enumerate(zip(held, dsts))]
    for load in loads:
        load.start()
    for load, store in zip(loads, stores):
        load.wait()
        store.start()
    for store in stores:
        store.wait()


def per_device(inputs, out_grad, weight, moment_mean, moment_square):
    dma = pltpu.SemaphoreType.DMA
    shape = jax.ShapeDtypeStruct
    hbm = pl.BlockSpec(memory_space=pl.ANY)
    small = shape((ROWS, COLS), F32)
    results = (shape((64, COLS), F32), shape((64, 1536), F32), small, small, small)

    def f32(*dims):
        return pltpu.VMEM(dims, F32)

    staged = [f32(*result.shape) for result in results]

    done = pl.pallas_call(
        kernel,
        out_shape=results,
        in_specs=[hbm] * 5,
        out_specs=[hbm] * 5,
        scratch_shapes=[
            *staged,
            f32(SLAB, COLS),
            f32(NZ, SLAB, CA),
            f32(NH, 12, ROWS, CB),
            f32(NZ, SLAB, CA),
            f32(NH, NZ, ROWS, CB),
            f32(2, HALF, SLAB, CA),
            f32(2, HALF, ROWS, CB),
            f32(2, NZ, ROWS, CB),
            f32(NZ, ROWS, CB),
            f32(2, HALF, ROWS, CB),
            f32(SLAB, CA),
            f32(2, 16, CA),
            f32(2, ROWS, CA),
            f32(256, COLS),
            f32(2, 64, 256),
            f32(2, 64, COLS),
            f32(NZ, 2, 2, 64, 128),
            f32(NZ, 2, 64, 128),
            f32(NZ, 64, 128),
            f32(256, 1536), f32(256, COLS), f32(ROWS, COLS), f32(ROWS, COLS), f32(ROWS, COLS),
            pltpu.VMEM((256, 1536), BF16),
            pltpu.VMEM((256, 1536), BF16),
            pltpu.VMEM((256, COLS), BF16),
            pltpu.VMEM((256, COLS), BF16),
            dma((5,)), dma((5,)),
            dma((COPIES,)), dma((COPIES,)),
            dma((NZ,)), dma((NZ,)),
            dma((NZ,)), dma((NZ,)),
        ],
        compiler_params=pltpu.CompilerParams(
            collective_id=0, has_side_effects=True, vmem_limit_bytes=67043328
        ),
        name="step",
    )(inputs, out_grad, weight, moment_mean, moment_square)
    return pl.pallas_call(
        write,
        out_shape=results,
        in_specs=[hbm] * 5,
        out_specs=[hbm] * 5,
        scratch_shapes=[*staged, dma((5,)), dma((5,))],
        compiler_params=pltpu.CompilerParams(vmem_limit_bytes=67043328),
        name="write",
    )(*done)


def solution(mesh):
    split = Mesh(mesh.devices.reshape(NZ, NH, NX, 2, 2), ("z", "h", "x", "l", "c"))
    tile = P(("x", "z", "h"), ("l", "c"))
    return jax.shard_map(
        per_device,
        mesh=split,
        in_specs=(P(("z", "h"), "x"), P(("z", "h"), ("l", "c")), tile, tile, tile),
        out_specs=(P(("z", "h", "x"), ("l", "c")), P(("z", "h", "l", "c"), "x"), tile, tile, tile),
        check_vma=False,
    )
```

time: 199 us -> 94.3 us (0.47)
  waiting for transfers between devices: 152 us -> 0 us
  Pallas kernels: 0 us -> 92.3 us
  matrix products: 15.9 us -> 0 us
  between operations: 15.2 us -> 0.64 us
  blocking collectives: 10.5 us -> 0 us
  other arithmetic: 2.23 us -> 0 us
    pallas_call x0 -> x2, Pallas kernels: none -> 92.3 us  [the longest x1 90.3 us: per_device(): pl.pallas_call(kernel, out_shape=results, in_specs=[hbm] * 5, out_specs=[...]
    reduce_scatter x3 -> x0, waiting for transfers between devices: 84.7 us -> none  [the longest x2 72.4 us: sum_by_axis(): subtotal = lax.psum_scatter(subtotal, axis, scatter_dimension=0, tiled=True)]
    all_gather x1 -> x0, waiting for transfers between devices: 66.9 us -> none  [per_device(): weight_tile = lax.all_gather(weight, DP, axis=0, tiled=True)]
    dot_general x3 -> x0, matrix products: 15.9 us -> none  [the longest x1 5.83 us: per_device(): lax.dot_general(out_grad, weight_tile, (((1,), (1,)), ((), ())), precisio...]
    all_to_all x1 -> x0, blocking collectives: 10.5 us -> none  [summed_on_arrival(): tiles = lax.all_to_all(cut_along(array, dim, count), axis, 0, 0, tiled=True)]
  transfers between devices with their start and end apart: 4 -> 0, of which waited for: 3 -> 0; matrix products, arithmetic and copies ran while one was open for 6% -> 0% of each run, Pallas kernels for 0% -> 0%
where the time goes in v2:
time: 94.3 us; the launch traced here: 92.9 us
  Pallas kernels  92.3 us (98%)
    pallas_call x1, Pallas kernels, per_device(): pl.pallas_call(kernel, out_shape=results, in_specs=[hbm] * 5, out_specs=[...  90.3 us
    pallas_call x1, Pallas kernels, per_device(): pl.pallas_call(write, out_shape=results, in_specs=[hbm] * 5, out_specs=[h...  1.96 us

profile of v2, /device:TPU:6, one launch (start us, length us, event | category | flops | bytes accessed | tf_op | source)
XLA Modules:
  0.0 92.9 jit_solution(11225363176979250538)
XLA Ops:
  0.6 90.3 %step.1 = (f32[64,512]{1,0:T(8,128)}, f32[64,1536]{1,0:T(8,128)}, f32[32,512]{1,0:T(8,128)}, f32[32,512]{1,0:T(8,128)}, f32[32,512]{1,0:T(8,128)}) custom-call(f32[256,1536]{1,0:T(8,128)} %in_hbm.1, f32[256,512]{1,0:T(8,128)} %og_hbm.1, f32[32,512]{1,0:T(8,128)} %w_hbm.1, f32[32,512]{1,0:T(8,128)} %mm_hbm.1, f32[32,512]{1,0:T(8,128)} %ms_hbm.1), custom_call_target="tpu_custom_call" | custom-call | tf_op jit(solution)/shard_map/step/pallas_call | solution.py:464
  91.0 2.0 %write.1 = (f32[64,512]{1,0:T(8,128)}, f32[64,1536]{1,0:T(8,128)}, f32[32,512]{1,0:T(8,128)}, f32[32,512]{1,0:T(8,128)}, f32[32,512]{1,0:T(8,128)}) custom-call(f32[64,512]{1,0:T(8,128)} %get-tuple-element.10.refs_0_, f32[64,1536]{1,0:T(8,128)} %get-tuple-element.11.refs_1_, f32[32,512]{1,0:T(8,128)} %get-tuple-element.12.refs_2_, ...), custom_call_target="tpu_custom_call" | custom-call | tf_op jit(solution)/shard_map/write/pallas_call | solution.py:505

commit v3 on v2

--- a/solution.py
+++ b/solution.py
@@ -11,15 +11,14 @@
 STEP = 10
 NZ, NH, NX = 12, 4, 4
 HALF = NZ // 2
-ORDER = (0, 1, 3, 2)
-LAST = ((0, 1), (3, 2))
 MESH = pl.DeviceIdType.MESH
 ROWS = 32
 SLAB = NH * ROWS
 COLS = 512
 CA = 384
 CB = COLS - CA
-COPIES = 160
+ARRIVALS = 103
+SENDS = 11
 F32 = jnp.float32
 BF16 = jnp.bfloat16
 
@@ -52,8 +51,8 @@
     out_hbm, ig_hbm, nw_hbm, nm_hbm, ns_hbm,
     out_ref, ig_ref, nw_ref, nm_ref, ns_ref,
     w0, wa, wb, pa, pb, rs, far_l, near_l, q, zb, total, tg, ga, pout, tx, xl, pin, cland, yland,
-    in_v, og_v, w_v, mm_v, ms_v, in_hi, in_lo, og_hi, og_lo,
-    l_sem, o_sem, s_sem, r_sem, c_s, c_r, y_s, y_r,
+    in_v, og_v, w_v, mm_v, ms_v, in_hi, in_lo, og3,
+    l_sem, o_sem, s_sem, r_sem, c_r, y_r,
 ):
     z, h, x = lax.axis_index("z"), lax.axis_index("h"), lax.axis_index("x")
     l, c = lax.axis_index("l"), lax.axis_index("c")
@@ -75,11 +74,16 @@
             src_ref=src, dst_ref=dst, send_sem=s, recv_sem=r, device_id=dev, device_id_type=MESH
         )
 
-    made = []
-
-    def copy(src, dst, dev):
-        made.append(remote(src, dst, s_sem.at[len(made)], r_sem.at[len(made)], dev))
-        return made[-1]
+    arrivals = []
+
+    def arrival():
+        arrivals.append(len(arrivals))
+        return arrivals[-1]
+
+    H_SENT, A_SENT, B_SENT, BH_SENT, R_SENT, G_SENT, Q_SENT, X_SENT, T_SENT, C_SENT, Y_SENT = range(SENDS)
+
+    def copy(src, dst, dev, sent, at=None):
+        return remote(src, dst, s_sem.at[sent], r_sem.at[arrival() if at is None else at], dev)
 
     loads = [
         pltpu.make_async_copy(a, b, l_sem.at[n])
@@ -108,34 +112,42 @@
 
     cols_a, cols_b = pl.ds(0, CA), pl.ds(CA, CB)
 
-    own_h = {j: copy(w_hbm, w0.at[rows_of(h)], hto(j)) for j in (1, 3, 2)}
-    ag = {}
-    for i in range(HALF):
-        for d in (0, 1):
-            zz = zz_at(-sign(d) * i)
-            for k in ORDER:
-                if i < HALF - 1 or k in LAST[d]:
-                    at = rows_of(around(h, -k, NH))
-                    src = wa.at[zz, at]
-                    if i == 0:
-                        src = w_hbm.at[:, cols_a] if k == 0 else w0.at[at, cols_a]
-                    ag[d, i, k] = copy(src, wa.at[zz, at], zto(sign(d)))
+    own_h = {j: copy(w_hbm, w0.at[rows_of(h)], hto(j), H_SENT) for j in (1, 3, 2)}
+    ag, came = {}, {}
+    for d in (0, 1):
+        for k in range(NH):
+            at = rows_of(around(h, -k, NH))
+            src = w_hbm.at[:, cols_a] if k == 0 else w0.at[at, cols_a]
+            ids = arrival()
+            came[d] = ids - k
+            ag[d, 0, k] = copy(src, wa.at[z, at], zto(sign(d)), A_SENT, ids)
+    near_half = h // 2
+
+    def half_of(r):
+        return pl.ds(pl.multiple_of((near_half if r == 0 else 1 - near_half) * 64, 64), 64)
+
+    for i in range(1, HALF):
+        for d in (0, 1):
+            for r in (0, 1):
+                if i < HALF - 1 or r == d:
+                    here = wa.at[zz_at(-sign(d) * i), half_of(r)]
+                    ag[d, i, r] = copy(here, here, zto(sign(d)), A_SENT)
 
     bz = {}
     for i in range(HALF):
         for d in (0, 1):
             if i < HALF - 1 or d == 0:
                 src = w_hbm.at[:, cols_b] if i == 0 else wb.at[h, place(d, i)]
-                bz[d, i] = copy(src, wb.at[h, place(d, i + 1)], zto(sign(d)))
+                bz[d, i] = copy(src, wb.at[h, place(d, i + 1)], zto(sign(d)), B_SENT)
     bh, bf = {}, {}
     for b in range(3):
         n = 4 if b < 2 else 3
         for d in (0, 1):
             at = pl.ds(1 + 4 * b, n)
-            bh[b, d] = copy(wb.at[h, at], wb.at[h, at], hto(sign(d)))
+            bh[b, d] = copy(wb.at[h, at], wb.at[h, at], hto(sign(d)), BH_SENT)
             at = pl.ds(1 + 4 * b + 2 * d, 2 if d == 0 else n - 2)
             back = around(h, -sign(d), NH)
-            bf[b, d] = copy(wb.at[back, at], wb.at[back, at], hto(sign(d)))
+            bf[b, d] = copy(wb.at[back, at], wb.at[back, at], hto(sign(d)), BH_SENT)
 
     def bhop(i):
         for d in (0, 1):
@@ -151,22 +163,22 @@
                 if i > 0 or half == d:
                     at = pl.ds(half * 64, 64)
                     src = pa.at[0, at] if i == 0 else rs.at[d, i - 1, at]
-                    rsa[d, i, half] = copy(src, rs.at[d, i, at], zto(sign(d)))
+                    rsa[d, i, half] = copy(src, rs.at[d, i, at], zto(sign(d)), R_SENT)
 
     groups = (pl.ds(0, HALF), pl.ds(HALF, HALF))
     two = around(h, 2, NH)
-    g_far = {d: copy(pb.at[two, groups[d]], far_l.at[d], hto(sign(d))) for d in (0, 1)}
+    g_far = {d: copy(pb.at[two, groups[d]], far_l.at[d], hto(sign(d)), G_SENT) for d in (0, 1)}
     g_near = {}
     for d in (0, 1):
         to = around(h, sign(d), NH)
         for g in (0, 1):
-            g_near[d, g] = copy(pb.at[to, groups[g]], near_l.at[d, groups[g]], hto(sign(d)))
+            g_near[d, g] = copy(pb.at[to, groups[g]], near_l.at[d, groups[g]], hto(sign(d)), G_SENT)
     rz = {}
     for j in range(HALF):
         for d in (0, 1):
             if j >= d:
                 src = q.at[0 if d == 0 else NZ - 1] if j == d else zb.at[d, j - 1]
-                rz[d, j] = copy(src, zb.at[d, j], zto(sign(d)))
+                rz[d, j] = copy(src, zb.at[d, j], zto(sign(d)), Q_SENT)
 
     def rhop(j):
         for d in (0, 1):
@@ -186,11 +198,12 @@
     for load in loads[:3]:
         load.wait()
     w0[rows_of(h), :] = w_v[...]
-    og_hi[...], og_lo[...] = halves(og_v[...])
+    high, low = halves(og_v[...])
+    og3[...] = jnp.concatenate([high, high, low], axis=1)
     in_hi[...], in_lo[...] = halves(in_v[...])
 
     def og():
-        return og_hi[...], og_lo[...]
+        return og3[:, :COLS], og3[:, 2 * COLS :]
 
     def product(s):
         at = lanes_of(zz_at(HALF - s))
@@ -199,36 +212,39 @@
         pb[:, s] = part[:, CA:].reshape(NH, ROWS, CB)
 
     def c_copy(zz):
-        return remote(pin.at[zz, :, 1 - c], cland.at[zz], c_s.at[zz], c_r.at[zz], {"c": 1 - c})
+        return remote(pin.at[zz, :, 1 - c], cland.at[zz], s_sem.at[C_SENT], c_r.at[zz], {"c": 1 - c})
 
     def y_copy(zz):
-        return remote(pin.at[zz, 1 - l, c], yland.at[zz], y_s.at[zz], y_r.at[zz], {"l": 1 - l})
-
-    def multiply(zz, tile, start):
-        w = halves(tile)
-        part = dot3(og(), w, ((1,), (1,)))
-        pin[zz] = part.reshape(2, 2, 64, 128)
-        c_copy(zz).start()
-        at = lanes_of(zz)
-        out = dot3((in_hi[:, at], in_lo[:, at]), w, ((1,), (0,)))
+        return remote(pin.at[zz, 1 - l, c], yland.at[zz], s_sem.at[Y_SENT], y_r.at[0], {"l": 1 - l})
+
+    def multiply(parts, start=False):
+        across, down, left = [], [], []
+        for zz, tile in parts:
+            high, low = halves(tile)
+            at = lanes_of(zz)
+            across.append(jnp.concatenate([high, low, high], axis=1))
+            down += [high, low, high]
+            left += [in_hi[:, at], in_hi[:, at], in_lo[:, at]]
+        part = lax.dot_general(
+            og3[...], jnp.concatenate(across, axis=0), (((1,), (1,)), ((), ())), preferred_element_type=F32
+        )
+        for n, (zz, _) in enumerate(parts):
+            pin[zz] = part[:, n * SLAB : (n + 1) * SLAB].reshape(2, 2, 64, SLAB)
+            c_copy(zz).start()
+        out = jnp.dot(
+            jnp.concatenate(left, axis=1), jnp.concatenate(down, axis=0), preferred_element_type=F32
+        )
         pout[...] = out if start else pout[...] + out
 
-    def slab(by, at):
-        zz = zz_at(by)
-        tile = jnp.concatenate([wa[zz], wb[:, at].reshape(SLAB, CB)], axis=1)
-        multiply(zz, tile, False)
-
-    def slabs(first, last):
-        def each(n, carry):
-            i, d = first + n // 2, n % 2
-            slab((2 * d - 1) * i, 1 + 4 * ((i - 1) // 2) + 2 * d + (i - 1) % 2)
-            return carry
-
-        lax.fori_loop(0, 2 * (last - first + 1), each, 0)
+    def tile_of(zz, at):
+        return jnp.concatenate([wa[zz], wb[:, at].reshape(SLAB, CB)], axis=1)
+
+    def pair(i):
+        both = [zz_at(-sign(d) * i) for d in (0, 1)]
+        multiply([(zz, tile_of(zz, place(d, i))) for d, zz in enumerate(both)])
 
     def second(zz):
         c_copy(zz).wait_recv()
-        c_copy(zz).wait_send()
         pin[zz, 1 - l, c] = pin[zz, 1 - l, c] + cland[zz, 1 - l]
         y_copy(zz).start()
 
@@ -239,12 +255,17 @@
 
         lax.fori_loop(0, 2 * (last - first + 1), each, 0)
 
-    def ag_step(i, k):
-        for d in (0, 1):
-            if (d, i - 1, k) in ag:
-                ag[d, i - 1, k].wait_recv()
-                if (d, i, k) in ag:
-                    ag[d, i, k].start()
+    def ag_step(i, r):
+        for d in (0, 1):
+            if i == 1:
+                odd = h % 2
+                for k in (0, 3 - 2 * odd) if r == 0 else (1 + 2 * odd, 2):
+                    piece = wa.at[z, rows_of(0)]
+                    remote(piece, piece, s_sem.at[A_SENT], r_sem.at[came[d] + k], zto(1)).wait_recv()
+            elif (d, i - 1, r) in ag:
+                ag[d, i - 1, r].wait_recv()
+            if (d, i, r) in ag and i > 0:
+                ag[d, i, r].start()
 
     def rs_step(i):
         for half in (0, 1):
@@ -258,53 +279,55 @@
                     rs[d, i - 1, at, :] = mine
                 rsa[d, i, half].start()
 
+    def both(copies):
+        for d in (0, 1):
+            copies[d].start()
+
+    def over_h(b):
+        for d in (0, 1):
+            bh[b, d].wait_recv()
+            bf[b, d].start()
+
+    def piece(k):
+        own_h[k].wait_recv()
+        for d in (0, 1):
+            ag[d, 0, k].start()
+
     product(0)
     rsa[0, 0, 0].start()
     rsa[1, 0, 1].start()
-    for n, k in enumerate((1, 3, 2)):
-        own_h[k].wait_recv()
-        for d in (0, 1):
-            ag[d, 0, k].start()
-        product(1 + n)
-        product(NZ - 1 - n)
     bhop(1)
+    product(1)
+    product(NZ - 1)
+    piece(1)
+    product(2)
+    product(NZ - 2)
+    bhop(2)
+    for d in (0, 1):
+        bh[0, d].start()
+    piece(3)
+    product(3)
+    product(NZ - 3)
+    rs_step(1)
+    product(4)
+    product(NZ - 4)
+    product(5)
+    product(NZ - 5)
+    product(6)
+    both(g_far)
+    for d in (0, 1):
+        g_near[d, 1 - d].start()
+    bhop(3)
+    piece(2)
     ag_step(1, 0)
+    over_h(0)
     ag_step(1, 1)
-    product(4)
-    product(8)
-    ag_step(1, 3)
-    ag_step(1, 2)
-    rs_step(1)
-    bhop(2)
-    for d in (0, 1):
-        bh[0, d].start()
-    product(5)
-    product(7)
-    product(6)
-    for d in (0, 1):
-        g_far[d].start()
-    for d in (0, 1):
-        g_near[d, 1 - d].start()
-    multiply(z, w0[...], True)
+    bhop(4)
+    for d in (0, 1):
+        bh[1, d].start()
+    multiply([(z, w0[...])], True)
 
     for i in range(2, HALF):
-        if i <= 3:
-            bhop(2 * i - 1)
-        if i <= 4:
-            for d in (0, 1):
-                bh[i - 2, d].wait_recv()
-                bf[i - 2, d].start()
-        if i == 3:
-            for d in (0, 1):
-                for g in (0, 1):
-                    g_near[d, g].wait_recv()
-            g_near[0, 0].wait_send()
-            g_near[1, 1].wait_send()
-            q[...] = pb[h] + near_l[0] + near_l[1]
-        if i >= 3:
-            rhop(2 * (i - 3))
-        for k in ORDER:
-            ag_step(i, k)
         rs_step(i)
         if i == 2:
             for d in (0, 1):
@@ -312,80 +335,100 @@
                 to = around(h, sign(d), NH)
                 pb[to, groups[d]] = pb[to, groups[d]] + far_l[d]
                 g_near[d, d].start()
+        for r in (0, 1):
+            ag_step(i, r)
         if i <= 3:
-            bhop(2 * i)
+            bhop(i + 3)
+        if i >= 3:
+            rhop(i - 2)
+        if i == 2:
+            over_h(1)
             for d in (0, 1):
-                bh[i - 1, d].start()
-        if i >= 3:
-            rhop(2 * (i - 3) + 1)
+                bf[0, d].wait_recv()
+            second(z)
+            pair(1)
+            pair(2)
             for d in (0, 1):
-                bf[i - 3, d].wait_recv()
+                for g in (0, 1):
+                    g_near[d, g].wait_recv()
+            q[...] = pb[h] + near_l[0] + near_l[1]
+            rhop(0)
         if i == 3:
-            second(z)
-            slabs(1, 2)
+            for d in (0, 1):
+                bh[2, d].start()
+                bf[1, d].wait_recv()
+            seconds(1, 2)
+            pair(3)
         if i == 4:
-            seconds(1, 2)
-            slabs(3, 4)
+            over_h(2)
+            seconds(3, 3)
+            pair(4)
         if i == 5:
-            seconds(3, 4)
-            slabs(5, 5)
-
-    for k in ORDER:
-        ag_step(HALF, k)
-    slab(HALF, place(0, HALF))
+            for d in (0, 1):
+                bf[2, d].wait_recv()
+            seconds(4, 4)
+            pair(5)
+
+    for half in (0, 1):
+        at = pl.ds(half * 64, 64)
+        for d in (0, 1):
+            rsa[d, HALF - 1, half].wait_recv()
+        total[at, :] = pa[HALF, at, :] + rs[0, HALF - 1, at, :] + rs[1, HALF - 1, at, :]
+
+    def part_of(by, g):
+        return pl.ds(pl.multiple_of(around(h, by, NH) * ROWS + g * 16, 16), 16)
+
+    t_far = {d: copy(total.at[part_of(2, d)], tg.at[d], hto(sign(d)), T_SENT) for d in (0, 1)}
+    t_near = {}
+    for d in (0, 1):
+        for g in (0, 1):
+            t_near[d, g] = copy(
+                total.at[part_of(sign(d), g)], ga.at[d, pl.ds(g * 16, 16)], hto(sign(d)), T_SENT
+            )
+    both(t_far)
+    for d in (0, 1):
+        t_near[d, 1 - d].start()
+
+    for r in (0, 1):
+        ag_step(HALF, r)
+    far = zz_at(HALF)
+    multiply([(far, tile_of(far, place(0, HALF)))])
 
     def block(by):
         return pl.ds(pl.multiple_of(around(x, by, NX) * 64, 64), 64)
 
     sides = (pl.ds(0, 256), pl.ds(256, 256))
-    x_far = {d: copy(pout.at[block(2), sides[d]], tx.at[d], xto(sign(d))) for d in (0, 1)}
+    x_far = {d: copy(pout.at[block(2), sides[d]], tx.at[d], xto(sign(d)), X_SENT) for d in (0, 1)}
     x_near = {}
     for d in (0, 1):
         for g in (0, 1):
             x_near[d, g] = copy(
-                pout.at[block(sign(d)), sides[g]], xl.at[d, :, sides[g]], xto(sign(d))
+                pout.at[block(sign(d)), sides[g]], xl.at[d, :, sides[g]], xto(sign(d)), X_SENT
             )
     for d in (0, 1):
         x_far[d].start()
     for d in (0, 1):
         x_near[d, 1 - d].start()
 
-    for half in (0, 1):
-        at = pl.ds(half * 64, 64)
-        for d in (0, 1):
-            rsa[d, HALF - 1, half].wait_recv()
-        total[at, :] = pa[HALF, at, :] + rs[0, HALF - 1, at, :] + rs[1, HALF - 1, at, :]
-
-    def part_of(by, g):
-        return pl.ds(pl.multiple_of(around(h, by, NH) * ROWS + g * 16, 16), 16)
-
-    t_far = {d: copy(total.at[part_of(2, d)], tg.at[d], hto(sign(d))) for d in (0, 1)}
-    t_near = {}
-    for d in (0, 1):
-        for g in (0, 1):
-            t_near[d, g] = copy(
-                total.at[part_of(sign(d), g)], ga.at[d, pl.ds(g * 16, 16)], hto(sign(d))
-            )
-    for d in (0, 1):
-        t_far[d].start()
-    for d in (0, 1):
-        t_near[d, 1 - d].start()
-
-    far = zz_at(HALF)
+    rhop(4)
     seconds(5, 5)
     second(far)
-
+    for d in (0, 1):
+        t_far[d].wait_recv()
+        total[part_of(sign(d), d), :] = total[part_of(sign(d), d), :] + tg[d]
+        t_near[d, d].start()
     for d in (0, 1):
         x_far[d].wait_recv()
         pout[block(sign(d)), sides[d]] = pout[block(sign(d)), sides[d]] + tx[d]
         x_near[d, d].start()
-    for d in (0, 1):
-        t_far[d].wait_recv()
-        total[part_of(sign(d), d), :] = total[part_of(sign(d), d), :] + tg[d]
-        t_near[d, d].start()
+    rhop(5)
+
+    def taken(ref, sem):
+        pltpu.make_async_copy(ref, ref, sem).wait()
+
+    taken(yland, y_r.at[0])
 
     def finish(zz, carry):
-        y_copy(zz).wait()
         at = lanes_of(zz)
         ig_ref[:, at] = pin[zz, l, c] + cland[zz, l] + yland[zz]
         return carry
@@ -429,9 +472,22 @@
     for store in stores[2:]:
         store.start()
 
-    for one in made:
-        if one is not g_near[0, 0] and one is not g_near[1, 1]:
-            one.wait_send()
+    most = pl.ds(0, NZ - 1)
+    for sent, ref in (
+        (H_SENT, pout.at[pl.ds(0, 3 * ROWS)]),
+        (A_SENT, wa.at[most]),
+        (B_SENT, q.at[most]),
+        (BH_SENT, pb.at[pl.ds(0, 3), most]),
+        (R_SENT, pa.at[most]),
+        (G_SENT, pb.at[pl.ds(0, 3)]),
+        (Q_SENT, q.at[most]),
+        (X_SENT, pout.at[pl.ds(0, 192)]),
+        (T_SENT, total.at[pl.ds(0, 96)]),
+        (C_SENT, cland),
+        (Y_SENT, yland),
+    ):
+        taken(ref, s_sem.at[sent])
+    assert len(arrivals) == ARRIVALS, len(arrivals)
     for store in stores:
         store.wait()
 
@@ -490,12 +546,10 @@
             f32(256, 1536), f32(256, COLS), f32(ROWS, COLS), f32(ROWS, COLS), f32(ROWS, COLS),
             pltpu.VMEM((256, 1536), BF16),
             pltpu.VMEM((256, 1536), BF16),
-            pltpu.VMEM((256, COLS), BF16),
-            pltpu.VMEM((256, COLS), BF16),
+            pltpu.VMEM((256, 3 * COLS), BF16),
             dma((5,)), dma((5,)),
-            dma((COPIES,)), dma((COPIES,)),
-            dma((NZ,)), dma((NZ,)),
-            dma((NZ,)), dma((NZ,)),
+            dma((SENDS,)), dma((ARRIVALS,)),
+            dma((NZ,)), dma((1,)),
         ],
         compiler_params=pltpu.CompilerParams(
             collective_id=0, has_side_effects=True, vmem_limit_bytes=67043328

time: 94.3 us -> 85.6 us (0.908)
  Pallas kernels: 92.3 us -> 84.3 us
    pallas_call x1, Pallas kernels: 90.3 us -> 82.3 us  [per_device(): pl.pallas_call(kernel, out_shape=results, in_specs=[hbm] * 5, out_specs=[...]
where the time goes in v3:
time: 85.6 us; the launch traced here: 84.9 us
  Pallas kernels  84.3 us (98%)
    pallas_call x1, Pallas kernels, per_device(): pl.pallas_call(kernel, out_shape=results, in_specs=[hbm] * 5, out_specs=[...  82.3 us
    pallas_call x1, Pallas kernels, per_device(): pl.pallas_call(write, out_shape=results, in_specs=[hbm] * 5, out_specs=[h...  1.96 us

profile of v3, /device:TPU:6, one launch (start us, length us, event | category | flops | bytes accessed | tf_op | source)
XLA Modules:
  0.0 84.9 jit_solution(10902277630985484187)
XLA Ops:
  0.6 82.3 %step.1 = (f32[64,512]{1,0:T(8,128)}, f32[64,1536]{1,0:T(8,128)}, f32[32,512]{1,0:T(8,128)}, f32[32,512]{1,0:T(8,128)}, f32[32,512]{1,0:T(8,128)}) custom-call(f32[256,1536]{1,0:T(8,128)} %in_hbm.1, f32[256,512]{1,0:T(8,128)} %og_hbm.1, f32[32,512]{1,0:T(8,128)} %w_hbm.1, f32[32,512]{1,0:T(8,128)} %mm_hbm.1, f32[32,512]{1,0:T(8,128)} %ms_hbm.1), custom_call_target="tpu_custom_call" | custom-call | tf_op jit(solution)/shard_map/step/pallas_call | solution.py:520
  82.9 2.0 %write.1 = (f32[64,512]{1,0:T(8,128)}, f32[64,1536]{1,0:T(8,128)}, f32[32,512]{1,0:T(8,128)}, f32[32,512]{1,0:T(8,128)}, f32[32,512]{1,0:T(8,128)}) custom-call(f32[64,512]{1,0:T(8,128)} %get-tuple-element.10.refs_0_, f32[64,1536]{1,0:T(8,128)} %get-tuple-element.11.refs_1_, f32[32,512]{1,0:T(8,128)} %get-tuple-element.12.refs_2_, ...), custom_call_target="tpu_custom_call" | custom-call | tf_op jit(solution)/shard_map/write/pallas_call | solution.py:559

commit v4 on v3

--- a/solution.py
+++ b/solution.py
@@ -156,12 +156,15 @@
                 if (d, i) in bz:
                     bz[d, i].start()
 
+    def rows_in(r):
+        return half_of(1 - r)
+
     rsa = {}
     for i in range(HALF):
         for d in (0, 1):
             for half in (0, 1):
                 if i > 0 or half == d:
-                    at = pl.ds(half * 64, 64)
+                    at = rows_in(half)
                     src = pa.at[0, at] if i == 0 else rs.at[d, i - 1, at]
                     rsa[d, i, half] = copy(src, rs.at[d, i, at], zto(sign(d)), R_SENT)
 
@@ -267,17 +270,16 @@
             if (d, i, r) in ag and i > 0:
                 ag[d, i, r].start()
 
-    def rs_step(i):
-        for half in (0, 1):
-            for d in (0, 1):
-                at = pl.ds(half * 64, 64)
-                mine = pa[i if d == 0 else NZ - i, at, :]
-                if (d, i - 1, half) in rsa:
-                    rsa[d, i - 1, half].wait_recv()
-                    rs[d, i - 1, at, :] = rs[d, i - 1, at, :] + mine
-                else:
-                    rs[d, i - 1, at, :] = mine
-                rsa[d, i, half].start()
+    def rs_step(i, half):
+        for d in (0, 1):
+            at = rows_in(half)
+            mine = pa[i if d == 0 else NZ - i, at, :]
+            if (d, i - 1, half) in rsa:
+                rsa[d, i - 1, half].wait_recv()
+                rs[d, i - 1, at, :] = rs[d, i - 1, at, :] + mine
+            else:
+                rs[d, i - 1, at, :] = mine
+            rsa[d, i, half].start()
 
     def both(copies):
         for d in (0, 1):
@@ -296,81 +298,93 @@
     product(0)
     rsa[0, 0, 0].start()
     rsa[1, 0, 1].start()
+    for n in range(1, HALF):
+        product(n)
+        product(NZ - n)
+    product(HALF)
+    both(g_far)
+    for d in (0, 1):
+        g_near[d, 1 - d].start()
     bhop(1)
-    product(1)
-    product(NZ - 1)
     piece(1)
-    product(2)
-    product(NZ - 2)
     bhop(2)
-    for d in (0, 1):
-        bh[0, d].start()
     piece(3)
-    product(3)
-    product(NZ - 3)
-    rs_step(1)
-    product(4)
-    product(NZ - 4)
-    product(5)
-    product(NZ - 5)
-    product(6)
-    both(g_far)
-    for d in (0, 1):
-        g_near[d, 1 - d].start()
+    rs_step(1, 0)
+    rs_step(1, 1)
     bhop(3)
     piece(2)
     ag_step(1, 0)
-    over_h(0)
+    for d in (0, 1):
+        g_far[d].wait_recv()
+        to = around(h, sign(d), NH)
+        pb[to, groups[d]] = pb[to, groups[d]] + far_l[d]
+        g_near[d, d].start()
     ag_step(1, 1)
     bhop(4)
     for d in (0, 1):
-        bh[1, d].start()
+        bh[0, d].start()
     multiply([(z, w0[...])], True)
 
     for i in range(2, HALF):
-        rs_step(i)
-        if i == 2:
-            for d in (0, 1):
-                g_far[d].wait_recv()
-                to = around(h, sign(d), NH)
-                pb[to, groups[d]] = pb[to, groups[d]] + far_l[d]
-                g_near[d, d].start()
-        for r in (0, 1):
-            ag_step(i, r)
+        turns = {2: "rraa", 3: "rara", 4: "arar", 5: "aarr"}[i]
+        for n, turn in enumerate(turns):
+            (rs_step if turn == "r" else ag_step)(i, turns[:n].count(turn))
+            if n == 1 and i == 4:
+                for d in (0, 1):
+                    bf[0, d].wait_recv()
+                pair(1)
+                pair(2)
+            if n == 1 and i == 5:
+                seconds(1, 4)
         if i <= 3:
             bhop(i + 3)
-        if i >= 3:
-            rhop(i - 2)
+            for d in (0, 1):
+                bh[i - 1, d].start()
         if i == 2:
-            over_h(1)
-            for d in (0, 1):
-                bf[0, d].wait_recv()
-            second(z)
-            pair(1)
-            pair(2)
             for d in (0, 1):
                 for g in (0, 1):
                     g_near[d, g].wait_recv()
             q[...] = pb[h] + near_l[0] + near_l[1]
-            rhop(0)
+        rhop(i - 2)
+        if i == 2:
+            second(z)
         if i == 3:
-            for d in (0, 1):
-                bh[2, d].start()
-                bf[1, d].wait_recv()
-            seconds(1, 2)
-            pair(3)
+            over_h(0)
+            over_h(1)
         if i == 4:
             over_h(2)
-            seconds(3, 3)
+            for d in (0, 1):
+                bf[1, d].wait_recv()
+            pair(3)
             pair(4)
         if i == 5:
             for d in (0, 1):
                 bf[2, d].wait_recv()
-            seconds(4, 4)
             pair(5)
 
-    for half in (0, 1):
-        at = pl.ds(half * 64, 64)
+    for r in (0, 1):
+        ag_step(HALF, r)
+    far = zz_at(HALF)
+    multiply([(far, tile_of(far, place(0, HALF)))])
+
+    def block(by):
+        return pl.ds(pl.multiple_of(around(x, by, NX) * 64, 64), 64)
+
+    sides = (pl.ds(0, 256), pl.ds(256, 256))
+    x_far = {d: copy(pout.at[block(2), sides[d]], tx.at[d], xto(sign(d)), X_SENT) for d in (0, 1)}
+    x_near = {}
+    for d in (0, 1):
+        for g in (0, 1):
+            x_near[d, g] = copy(
+                pout.at[block(sign(d)), sides[g]], xl.at[d, :, sides[g]], xto(sign(d)), X_SENT
+            )
+    for d in (0, 1):
+        x_far[d].start()
+    for d in (0, 1):
+        x_near[d, 1 - d].start()
+
+    def add_up(half):
+        at = rows_in(half)
         for d in (0, 1):
             rsa[d, HALF - 1, half].wait_recv()
         total[at, :] = pa[HALF, at, :] + rs[0, HALF - 1, at, :] + rs[1, HALF - 1, at, :]
@@ -385,43 +399,24 @@
             t_near[d, g] = copy(
                 total.at[part_of(sign(d), g)], ga.at[d, pl.ds(g * 16, 16)], hto(sign(d)), T_SENT
             )
+    add_up(0)
     both(t_far)
+    add_up(1)
     for d in (0, 1):
         t_near[d, 1 - d].start()
-
-    for r in (0, 1):
-        ag_step(HALF, r)
-    far = zz_at(HALF)
-    multiply([(far, tile_of(far, place(0, HALF)))])
-
-    def block(by):
-        return pl.ds(pl.multiple_of(around(x, by, NX) * 64, 64), 64)
-
-    sides = (pl.ds(0, 256), pl.ds(256, 256))
-    x_far = {d: copy(pout.at[block(2), sides[d]], tx.at[d], xto(sign(d)), X_SENT) for d in (0, 1)}
-    x_near = {}
-    for d in (0, 1):
-        for g in (0, 1):
-            x_near[d, g] = copy(
-                pout.at[block(sign(d)), sides[g]], xl.at[d, :, sides[g]], xto(sign(d)), X_SENT
-            )
-    for d in (0, 1):
-        x_far[d].start()
-    for d in (0, 1):
-        x_near[d, 1 - d].start()
 
     rhop(4)
     seconds(5, 5)
     second(far)
-    for d in (0, 1):
-        t_far[d].wait_recv()
-        total[part_of(sign(d), d), :] = total[part_of(sign(d), d), :] + tg[d]
-        t_near[d, d].start()
     for d in (0, 1):
         x_far[d].wait_recv()
         pout[block(sign(d)), sides[d]] = pout[block(sign(d)), sides[d]] + tx[d]
         x_near[d, d].start()
     rhop(5)
+    for d in (0, 1):
+        t_far[d].wait_recv()
+        total[part_of(sign(d), d), :] = total[part_of(sign(d), d), :] + tg[d]
+        t_near[d, d].start()
 
     def taken(ref, sem):
         pltpu.make_async_copy(ref, ref, sem).wait()

time: 85.6 us -> 85.9 us (level)
  no operation moved by 1% of the time
where the time goes in v4:
time: 85.9 us; the launch traced here: 84.8 us
  Pallas kernels  84.2 us (98%)
    pallas_call x1, Pallas kernels, per_device(): pl.pallas_call(kernel, out_shape=results, in_specs=[hbm] * 5, out_specs=[...  82.2 us
    pallas_call x1, Pallas kernels, per_device(): pl.pallas_call(write, out_shape=results, in_specs=[hbm] * 5, out_specs=[h...  1.96 us

profile of v4, /device:TPU:6, one launch (start us, length us, event | category | flops | bytes accessed | tf_op | source)
XLA Modules:
  0.0 84.8 jit_solution(5157920696260091227)
XLA Ops:
  0.6 82.2 %step.1 = (f32[64,512]{1,0:T(8,128)}, f32[64,1536]{1,0:T(8,128)}, f32[32,512]{1,0:T(8,128)}, f32[32,512]{1,0:T(8,128)}, f32[32,512]{1,0:T(8,128)}) custom-call(f32[256,1536]{1,0:T(8,128)} %in_hbm.1, f32[256,512]{1,0:T(8,128)} %og_hbm.1, f32[32,512]{1,0:T(8,128)} %w_hbm.1, f32[32,512]{1,0:T(8,128)} %mm_hbm.1, f32[32,512]{1,0:T(8,128)} %ms_hbm.1), custom_call_target="tpu_custom_call" | custom-call | tf_op jit(solution)/shard_map/step/pallas_call | solution.py:515
  82.9 2.0 %write.1 = (f32[64,512]{1,0:T(8,128)}, f32[64,1536]{1,0:T(8,128)}, f32[32,512]{1,0:T(8,128)}, f32[32,512]{1,0:T(8,128)}, f32[32,512]{1,0:T(8,128)}) custom-call(f32[64,512]{1,0:T(8,128)} %get-tuple-element.10.refs_0_, f32[64,1536]{1,0:T(8,128)} %get-tuple-element.11.refs_1_, f32[32,512]{1,0:T(8,128)} %get-tuple-element.12.refs_2_, ...), custom_call_target="tpu_custom_call" | custom-call | tf_op jit(solution)/shard_map/write/pallas_call | solution.py:554

commit v5 on v3

--- a/solution.py
+++ b/solution.py
@@ -48,11 +48,10 @@
 
 def kernel(
     in_hbm, og_hbm, w_hbm, mm_hbm, ms_hbm,
-    out_hbm, ig_hbm, nw_hbm, nm_hbm, ns_hbm,
     out_ref, ig_ref, nw_ref, nm_ref, ns_ref,
     w0, wa, wb, pa, pb, rs, far_l, near_l, q, zb, total, tg, ga, pout, tx, xl, pin, cland, yland,
     in_v, og_v, w_v, mm_v, ms_v, in_hi, in_lo, og3,
-    l_sem, o_sem, s_sem, r_sem, c_r, y_r,
+    l_sem, s_sem, r_sem, c_r, y_r,
 ):
     z, h, x = lax.axis_index("z"), lax.axis_index("h"), lax.axis_index("x")
     l, c = lax.axis_index("l"), lax.axis_index("c")
@@ -156,12 +155,15 @@
                 if (d, i) in bz:
                     bz[d, i].start()
 
+    def rows_in(r):
+        return half_of(1 - r)
+
     rsa = {}
     for i in range(HALF):
         for d in (0, 1):
             for half in (0, 1):
                 if i > 0 or half == d:
-                    at = pl.ds(half * 64, 64)
+                    at = rows_in(half)
                     src = pa.at[0, at] if i == 0 else rs.at[d, i - 1, at]
                     rsa[d, i, half] = copy(src, rs.at[d, i, at], zto(sign(d)), R_SENT)
 
@@ -267,17 +269,16 @@
             if (d, i, r) in ag and i > 0:
                 ag[d, i, r].start()
 
-    def rs_step(i):
-        for half in (0, 1):
-            for d in (0, 1):
-                at = pl.ds(half * 64, 64)
-                mine = pa[i if d == 0 else NZ - i, at, :]
-                if (d, i - 1, half) in rsa:
-                    rsa[d, i - 1, half].wait_recv()
-                    rs[d, i - 1, at, :] = rs[d, i - 1, at, :] + mine
-                else:
-                    rs[d, i - 1, at, :] = mine
-                rsa[d, i, half].start()
+    def rs_step(i, half):
+        for d in (0, 1):
+            at = rows_in(half)
+            mine = pa[i if d == 0 else NZ - i, at, :]
+            if (d, i - 1, half) in rsa:
+                rsa[d, i - 1, half].wait_recv()
+                rs[d, i - 1, at, :] = rs[d, i - 1, at, :] + mine
+            else:
+                rs[d, i - 1, at, :] = mine
+            rsa[d, i, half].start()
 
     def both(copies):
         for d in (0, 1):
@@ -308,7 +309,8 @@
     piece(3)
     product(3)
     product(NZ - 3)
-    rs_step(1)
+    rs_step(1, 0)
+    rs_step(1, 1)
     product(4)
     product(NZ - 4)
     product(5)
@@ -328,15 +330,17 @@
     multiply([(z, w0[...])], True)
 
     for i in range(2, HALF):
-        rs_step(i)
+        turns = {2: "rr", 3: "rara", 4: "arar", 5: "aarr"}[i]
+        for n, turn in enumerate(turns):
+            (rs_step if turn == "r" else ag_step)(i, turns[:n].count(turn))
         if i == 2:
             for d in (0, 1):
                 g_far[d].wait_recv()
                 to = around(h, sign(d), NH)
                 pb[to, groups[d]] = pb[to, groups[d]] + far_l[d]
                 g_near[d, d].start()
-        for r in (0, 1):
-            ag_step(i, r)
+            ag_step(i, 0)
+            ag_step(i, 1)
         if i <= 3:
             bhop(i + 3)
         if i >= 3:
@@ -369,8 +373,29 @@
             seconds(4, 4)
             pair(5)
 
-    for half in (0, 1):
-        at = pl.ds(half * 64, 64)
+    for r in (0, 1):
+        ag_step(HALF, r)
+    far = zz_at(HALF)
+    multiply([(far, tile_of(far, place(0, HALF)))])
+
+    def block(by):
+        return pl.ds(pl.multiple_of(around(x, by, NX) * 64, 64), 64)
+
+    sides = (pl.ds(0, 256), pl.ds(256, 256))
+    x_far = {d: copy(pout.at[block(2), sides[d]], tx.at[d], xto(sign(d)), X_SENT) for d in (0, 1)}
+    x_near = {}
+    for d in (0, 1):
+        for g in (0, 1):
+            x_near[d, g] = copy(
+                pout.at[block(sign(d)), sides[g]], xl.at[d, :, sides[g]], xto(sign(d)), X_SENT
+            )
+    for d in (0, 1):
+        x_far[d].start()
+    for d in (0, 1):
+        x_near[d, 1 - d].start()
+
+    def add_up(half):
+        at = rows_in(half)
         for d in (0, 1):
             rsa[d, HALF - 1, half].wait_recv()
         total[at, :] = pa[HALF, at, :] + rs[0, HALF - 1, at, :] + rs[1, HALF - 1, at, :]
@@ -385,42 +410,23 @@
             t_near[d, g] = copy(
                 total.at[part_of(sign(d), g)], ga.at[d, pl.ds(g * 16, 16)], hto(sign(d)), T_SENT
             )
+    add_up(0)
     both(t_far)
+    add_up(1)
     for d in (0, 1):
         t_near[d, 1 - d].start()
-
-    for r in (0, 1):
-        ag_step(HALF, r)
-    far = zz_at(HALF)
-    multiply([(far, tile_of(far, place(0, HALF)))])
-
-    def block(by):
-        return pl.ds(pl.multiple_of(around(x, by, NX) * 64, 64), 64)
-
-    sides = (pl.ds(0, 256), pl.ds(256, 256))
-    x_far = {d: copy(pout.at[block(2), sides[d]], tx.at[d], xto(sign(d)), X_SENT) for d in (0, 1)}
-    x_near = {}
-    for d in (0, 1):
-        for g in (0, 1):
-            x_near[d, g] = copy(
-                pout.at[block(sign(d)), sides[g]], xl.at[d, :, sides[g]], xto(sign(d)), X_SENT
-            )
-    for d in (0, 1):
-        x_far[d].start()
-    for d in (0, 1):
-        x_near[d, 1 - d].start()
 
     rhop(4)
     seconds(5, 5)
     second(far)
     for d in (0, 1):
+        x_far[d].wait_recv()
+        pout[block(sign(d)), sides[d]] = pout[block(sign(d)), sides[d]] + tx[d]
+        x_near[d, d].start()
+    for d in (0, 1):
         t_far[d].wait_recv()
         total[part_of(sign(d), d), :] = total[part_of(sign(d), d), :] + tg[d]
         t_near[d, d].start()
-    for d in (0, 1):
-        x_far[d].wait_recv()
-        pout[block(sign(d)), sides[d]] = pout[block(sign(d)), sides[d]] + tx[d]
-        x_near[d, d].start()
     rhop(5)
 
     def taken(ref, sem):
@@ -434,13 +440,6 @@
         return carry
 
     lax.fori_loop(0, NZ, finish, 0)
-    stores = [
-        pltpu.make_async_copy(a, b, o_sem.at[n])
-        for n, (a, b) in enumerate(
-            ((ig_ref, ig_hbm), (out_ref, out_hbm), (nw_ref, nw_hbm), (nm_ref, nm_hbm), (ns_ref, ns_hbm))
-        )
-    ]
-    stores[0].start()
     for load in loads[3:]:
         load.wait()
 
@@ -463,14 +462,11 @@
         for g in (0, 1):
             x_near[d, g].wait_recv()
     out_ref[...] = pout[block(0), :] + xl[0] + xl[1]
-    stores[1].start()
 
     for d in (0, 1):
         for g in (0, 1):
             t_near[d, g].wait_recv()
     adamw(cols_a, total[rows_of(h), :] + ga[0] + ga[1])
-    for store in stores[2:]:
-        store.start()
 
     most = pl.ds(0, NZ - 1)
     for sent, ref in (
@@ -488,18 +484,12 @@
     ):
         taken(ref, s_sem.at[sent])
     assert len(arrivals) == ARRIVALS, len(arrivals)
+
+
+def write(*refs):
+    held, dsts, o_sem = refs[:5], refs[5:10], refs[10]
+    stores = [pltpu.make_async_copy(a, b, o_sem.at[n]) for n, (a, b) in enumerate(zip(held, dsts))]
     for store in stores:
-        store.wait()
-
-
-def write(*refs):
-    srcs, dsts, held, l_sem, o_sem = refs[:5], refs[5:10], refs[10:15], refs[15], refs[16]
-    loads = [pltpu.make_async_copy(a, b, l_sem.at[n]) for n, (a, b) in enumerate(zip(srcs, held))]
-    stores = [pltpu.make_async_copy(a, b, o_sem.at[n]) for n, (a, b) in enumerate(zip(held, dsts))]
-    for load in loads:
-        load.start()
-    for load, store in zip(loads, stores):
-        load.wait()
         store.start()
     for store in stores:
         store.wait()
@@ -515,15 +505,14 @@
     def f32(*dims):
         return pltpu.VMEM(dims, F32)
 
-    staged = [f32(*result.shape) for result in results]
+    vmem = pl.BlockSpec(memory_space=pltpu.VMEM)
 
     done = pl.pallas_call(
         kernel,
         out_shape=results,
         in_specs=[hbm] * 5,
-        out_specs=[hbm] * 5,
+        out_specs=[vmem] * 5,
         scratch_shapes=[
-            *staged,
             f32(SLAB, COLS),
             f32(NZ, SLAB, CA),
             f32(NH, 12, ROWS, CB),
@@ -547,22 +536,22 @@
             pltpu.VMEM((256, 1536), BF16),
             pltpu.VMEM((256, 1536), BF16),
             pltpu.VMEM((256, 3 * COLS), BF16),
-            dma((5,)), dma((5,)),
+            dma((5,)),
             dma((SENDS,)), dma((ARRIVALS,)),
             dma((NZ,)), dma((1,)),
         ],
         compiler_params=pltpu.CompilerParams(
-            collective_id=0, has_side_effects=True, vmem_limit_bytes=67043328
+            collective_id=0, has_side_effects=True, vmem_limit_bytes=48 << 20
         ),
         name="step",
-    )(inputs, out_grad, weight, moment_mean, moment_square)
+    )(*[pltpu.with_memory_space_constraint(a, pltpu.HBM) for a in (inputs, out_grad, weight, moment_mean, moment_square)])
     return pl.pallas_call(
         write,
         out_shape=results,
-        in_specs=[hbm] * 5,
-        out_specs=[hbm] * 5,
-        scratch_shapes=[*staged, dma((5,)), dma((5,))],
-        compiler_params=pltpu.CompilerParams(vmem_limit_bytes=67043328),
+        in_specs=[vmem] * 5,
+        out_specs=[pl.BlockSpec(memory_space=pltpu.HBM)] * 5,
+        scratch_shapes=[dma((5,))],
+        compiler_params=pltpu.CompilerParams(vmem_limit_bytes=1 << 20),
         name="write",
     )(*done)
 

time: 85.6 us -> 83.4 us (0.974)
  Pallas kernels: 84.3 us -> 82.6 us
    pallas_call x1, Pallas kernels: 1.96 us -> 0.89 us  [per_device(): pl.pallas_call(write, out_shape=results, in_specs=[vmem] * 5, out_specs=[...]
where the time goes in v5:
time: 83.4 us; the launch traced here: 83.2 us
  Pallas kernels  82.6 us (99%)
    pallas_call x1, Pallas kernels, per_device(): pl.pallas_call(kernel, out_shape=results, in_specs=[hbm] * 5, out_specs=[...  81.7 us

profile of v5, /device:TPU:6, one launch (start us, length us, event | category | flops | bytes accessed | tf_op | source)
XLA Modules:
  0.0 83.2 jit_solution(9638278293856939699)
XLA Ops:
  0.6 81.7 %step.1 = (f32[64,512]{1,0:T(8,128)S(1)}, f32[64,1536]{1,0:T(8,128)S(1)}, f32[32,512]{1,0:T(8,128)S(1)}, f32[32,512]{1,0:T(8,128)S(1)}, f32[32,512]{1,0:T(8,128)S(1)}) custom-call(f32[256,1536]{1,0:T(8,128)} %in_hbm.1, f32[256,512]{1,0:T(8,128)} %og_hbm.1, f32[32,512]{1,0:T(8,128)} %w_hbm.1, f32[32,512]{1,0:T(8,128)} %mm_hbm.1, f32[32,512]{1,0:T(8,128)} %ms_hbm.1), custom_call_target="tpu_custom_call" | custom-call | tf_op jit(solution)/shard_map/step/pallas_call | solution.py:510
  82.3 0.9 %write.1 = (f32[64,512]{1,0:T(8,128)}, f32[64,1536]{1,0:T(8,128)}, f32[32,512]{1,0:T(8,128)}, f32[32,512]{1,0:T(8,128)}, f32[32,512]{1,0:T(8,128)}) custom-call(f32[64,512]{1,0:T(8,128)S(1)} %get-tuple-element.10.refs_0_, f32[64,1536]{1,0:T(8,128)S(1)} %get-tuple-element.11.refs_1_, f32[32,512]{1,0:T(8,128)S(1)} %get-tuple-element.12.refs_2_, ...), custom_call_target="tpu_custom_call" | custom-call | tf_op jit(solution)/shard_map/write/pallas_call | solution.py:548
